TPU v7x, 128 devices: a whole 4x4x4 slice. The times are simulated.
128 devices in a mesh: ctx: 32 (over z_hi, x, y), kv: 4 (over z_lo, core).
Axes of the slice: x: 4, y: 4, z: 4 (z_hi: 2, z_lo: 2; z = z_hi * 2 + z_lo), core: 2. Of those that a mesh axis runs over, the one named last changes fastest.
Arguments:
- queries: bfloat16 [12288, 64, 128], P('ctx', 'kv'), may hold values from -128 to 128
- key_heads: bfloat16 [12288, 8, 128], P('ctx', 'kv'), may hold values from -6 to 6
- value_heads: bfloat16 [12288, 8, 128], P('ctx', 'kv'), may hold values from -6 to 6
- grad_out: bfloat16 [12288, 64, 128], P('ctx', 'kv'), may hold values from -6 to 6
- transforms: float32 [32, 128, 128], P('ctx'), may hold values from -1.2 to 1.2
- window: int32 [8], P('kv'), may hold values from 1 to 4, as said below
- first_block: int32 [1], replicated, may hold values from 0 to 31
Outputs:
- query_grad: bfloat16 [12288, 64, 128], P('ctx', 'kv')
- key_grad: bfloat16 [12288, 8, 128], P('ctx', 'kv')
- value_grad: bfloat16 [12288, 8, 128], P('ctx', 'kv')
- turn_grad: float32 [32, 128, 128], P('ctx')
Inputs may be any that keep to these rules, and one draw needn't show every extreme that they name: Some key-value head has a window of 4 blocks.
All inputs are finite; a program needn't handle non-finite values.
Results may differ from a plain program's by a relative error of at most 0.019.
Values may be sent and summed in bfloat16 or wider, within the bound.
No kernel may reach another device: no remote copies, remote signals or barrier semaphores. Data moves between devices by JAX's collectives and lax.ppermute only.
A program may use at most 256 MiB of HBM per device.

v0:
```python
import functools
import math

import jax
import jax.numpy as jnp
from jax import lax
from jax.experimental import pallas as pl
from jax.experimental.pallas import tpu as pltpu
from jax.sharding import PartitionSpec as P

HOPS = 3
F32 = jnp.float32
BF16 = jnp.bfloat16
LOG2E = math.log2(math.e)


def dot(a, b, ca, cb):
    return lax.dot_general(a, b, (((ca,), (cb,)), ((), ())), preferred_element_type=F32)


def dot_precise(a, b, ca, cb):
    return lax.dot_general(
        a, b, (((ca,), (cb,)), ((), ())), preferred_element_type=F32, precision=lax.Precision.HIGHEST
    )


def halves(x):
    upper = x.astype(BF16)
    return upper, (x - upper.astype(F32)).astype(BF16)


def shift(x, by):
    n = lax.axis_size("ctx")
    return lax.ppermute(x, "ctx", [(i, (i + by) % n) for i in range(n)])


def prepare(k_ref, v_ref, t_ref, a_ref, b_ref, own_ref, wide, *, n):
    d = k_ref.shape[-1]
    for part, src in enumerate((k_ref, v_ref)):
        wide[...] = src[...].astype(F32)
        for g, out in enumerate((a_ref, b_ref)):
            rows = wide[pl.ds(g, n, stride=2)].astype(BF16)
            out[part * n : (part + 1) * n] = rows
            own_ref[g, part * n : (part + 1) * n] = rows
    upper, lower = halves(t_ref[...])
    a_ref[2 * n : 2 * n + d] = upper
    a_ref[2 * n + d : 2 * n + 2 * d] = lower


def diagonal(s, first, group):
    key = lax.broadcasted_iota(jnp.int32, s.shape, 0)
    row = first + lax.broadcasted_iota(jnp.int32, s.shape, 1) // group
    return jnp.where(key <= row, s, -jnp.inf)


def near_stats(q_ref, do_ref, own_ref, stat_ref, *, n, d, cut, c2):
    group = q_ref.shape[1]
    for c in range(n // cut):
        lo, hi = c * cut, (c + 1) * cut
        q = q_ref[lo:hi].reshape(cut * group, d)
        do = do_ref[lo:hi].reshape(cut * group, d)
        s = diagonal(dot(own_ref[0:hi], q, 1, 1), lo, group)
        dp = dot(own_ref[n : n + hi], do, 1, 1)
        m = jnp.max(s, axis=0, keepdims=True)
        e = jnp.exp2((s - m) * c2)
        cols = slice(lo * group, hi * group)
        stat_ref[0:1, cols] = m
        stat_ref[1:2, cols] = jnp.sum(e, axis=0, keepdims=True)
        stat_ref[2:3, cols] = jnp.sum(e * dp, axis=0, keepdims=True)


def far(
    win, fst, q_ref, do_ref, r1_ref, r2_ref, r3_ref, t1_ref, t2_ref, t3_ref, near_ref, *rest,
    head, n, d, hops, c2, factor, blocks,
):
    if head:
        prev_dm, rest = rest[0], rest[3:]
    dq_ref, stat_ref, y1_ref, y2_ref, y3_ref = rest[0:5]
    dm_refs = rest[5:-9]
    prod, keys, vals, keys_t, dk, dv, e_ref, p_ref, tops = rest[-9:]
    group = q_ref.shape[1]
    R = n * group
    place = lax.rem(lax.axis_index("ctx") - fst[0] + blocks, blocks)
    live = jnp.minimum(win[head], place + 1) - 1
    sources = (r1_ref, r2_ref, r3_ref)
    turns = (t1_ref, t2_ref, t3_ref)

    dk[...] = jnp.zeros_like(dk)
    dv[...] = jnp.zeros_like(dv)
    total = None
    for i in range(hops):
        mat = turns[i][0:d].astype(F32) + turns[i][d : 2 * d].astype(F32)
        total = mat if total is None else dot_precise(total, mat, 1, 0)
        prod[i] = total
        upper, lower = halves(total)
        raw = sources[i][0:n]
        tile = (dot(raw, upper, 1, 1) + dot(raw, lower, 1, 1)).astype(BF16)
        keys[i] = tile
        keys_t[i] = tile.T
        vals[i] = sources[i][n : 2 * n]
    stat_ref[...] = near_ref[...]
    dq_ref[...] = jnp.zeros_like(dq_ref)

    def forward(i, carry):
        q = q_ref[...].reshape(R, d)
        do = do_ref[...].reshape(R, d)
        s = dot(keys[i], q, 1, 1)
        dp = dot(vals[i], do, 1, 1)
        m = stat_ref[0:1]
        m2 = jnp.maximum(m, jnp.max(s, axis=0, keepdims=True))
        e = jnp.exp2((s - m2) * c2)
        a = jnp.exp2((m - m2) * c2)
        stat_ref[1:2] = stat_ref[1:2] * a + jnp.sum(e, axis=0, keepdims=True)
        stat_ref[2:3] = stat_ref[2:3] * a + jnp.sum(e * dp, axis=0, keepdims=True)
        stat_ref[0:1] = m2
        tops[i] = m2
        e_ref[i] = e
        p_ref[i] = dp
        return carry

    lax.fori_loop(0, live, forward, 0)
    inv = 1.0 / stat_ref[1:2]
    stat_ref[1:2] = inv
    stat_ref[2:3] = stat_ref[2:3] * inv

    def backward(i, carry):
        q = q_ref[...].reshape(R, d)
        do = do_ref[...].reshape(R, d)
        w = e_ref[i] * (jnp.exp2((tops[i] - stat_ref[0:1]) * c2) * stat_ref[1:2])
        ds = (w * (p_ref[i] - stat_ref[2:3])).astype(BF16)
        dv[i] = dot(w.astype(BF16), do, 1, 0)
        dk[i] = dot(ds, q, 1, 0)
        dq_ref[...] += dot(keys_t[i], ds, 1, 0)
        return carry

    lax.fori_loop(0, live, backward, 0)

    grads = []
    for i, y_ref in enumerate((y1_ref, y2_ref, y3_ref)):
        g_up, g_lo = halves(dk[i] * factor)
        p_up, p_lo = halves(prod[i])
        back = dot(g_up, p_up, 1, 0) + dot(g_up, p_lo, 1, 0) + dot(g_lo, p_up, 1, 0)
        y_ref[0:n] = back.astype(BF16)
        y_ref[n : 2 * n] = dv[i].astype(BF16)
        raw = sources[i][0:n]
        grads.append(dot(g_up, raw, 0, 0) + dot(g_lo, raw, 0, 0))
    if head:
        t2, t3 = [t[0:d].astype(F32) + t[d : 2 * d].astype(F32) for t in turns[1:]]
        dm1, dm2, dm3 = [grads[i] + prev_dm[i] for i in range(3)]
        mid = dm2 + dot_precise(dm3, t3, 1, 1)
        dm_refs[0][...] = (dm1 + dot_precise(mid, t2, 1, 1)).astype(BF16)
        dm_refs[1][...] = dot_precise(prod[0], mid, 0, 0).astype(BF16)
        dm_refs[2][...] = dot_precise(prod[1], dm3, 0, 0).astype(BF16)
    else:
        for i in range(hops):
            dm_refs[0][i] = grads[i]


def near(q_ref, do_ref, own_ref, stat_ref, far_ref, dq_ref, y_ref, *, n, d, cut, c2, factor):
    group = q_ref.shape[1]
    keys_t = own_ref[0:n].T
    for c in reversed(range(n // cut)):
        lo, hi = c * cut, (c + 1) * cut
        cols = slice(lo * group, hi * group)
        q = q_ref[lo:hi].reshape(cut * group, d)
        do = do_ref[lo:hi].reshape(cut * group, d)
        s = diagonal(dot(own_ref[0:hi], q, 1, 1), lo, group)
        dp = dot(own_ref[n : n + hi], do, 1, 1)
        w = jnp.exp2((s - stat_ref[0:1, cols]) * c2) * stat_ref[1:2, cols]
        ds = (w * (dp - stat_ref[2:3, cols])).astype(BF16)
        dv = dot(w.astype(BF16), do, 1, 0)
        dk = dot(ds, q, 1, 0)
        if hi == n:
            y_ref[0:n] = dk
            y_ref[n : 2 * n] = dv
        else:
            y_ref[0:hi] += dk
            y_ref[n : n + hi] += dv
        dq = far_ref[:, cols] + dot(keys_t[:, 0:hi], ds, 1, 0)
        dq_ref[lo:hi] = (dq * factor).T.astype(BF16).reshape(cut, group, d)
    y_ref[0:n] = y_ref[0:n] * factor


def finish(own_ref, *refs, n):
    back = (refs[0:3], refs[3:6])
    outs = refs[6:8]
    wide = refs[8]
    for part in range(2):
        lo, hi = part * n, (part + 1) * n
        for g in range(2):
            total = own_ref[g, lo:hi]
            for b in back[g]:
                total = total + b[lo:hi].astype(F32)
            wide[pl.ds(g, n, stride=2)] = total
        outs[part][...] = wide[...].astype(BF16)


def whole(shape):
    return pl.BlockSpec(shape, lambda *a: (0,) * len(shape))


def cost(flops, size):
    return pl.CostEstimate(flops=flops, bytes_accessed=size, transcendentals=0)


def shards(queries, key_heads, value_heads, grad_out, transforms, window, first_block):
    n, heads, d = queries.shape
    kv = key_heads.shape[1]
    group = heads // kv
    R = n * group
    blocks = lax.axis_size("ctx")
    factor = 1.0 / math.sqrt(d)
    c2 = factor * LOG2E
    cut = n // 4
    q4 = queries.reshape(n, kv, group, d)
    do4 = grad_out.reshape(n, kv, group, d)

    buf_a, buf_b, own = pl.pallas_call(
        functools.partial(prepare, n=n),
        out_shape=[
            jax.ShapeDtypeStruct((2 * n + 2 * d, d), BF16),
            jax.ShapeDtypeStruct((2 * n, d), BF16),
            jax.ShapeDtypeStruct((kv, 2 * n, d), BF16),
        ],
        scratch_shapes=[pltpu.VMEM((2 * n, d), F32)],
        name="prepare",
    )(key_heads.reshape(2 * n, d), value_heads.reshape(2 * n, d), transforms[0])

    arr_a = []
    for h in range(1, HOPS + 1):
        arr_a.append(shift(buf_a, h))

    rows_blk = pl.BlockSpec((n, None, group, d), lambda g: (0, g, 0, 0))
    own_blk = pl.BlockSpec((None, 2 * n, d), lambda g: (g, 0, 0))
    stat_blk = pl.BlockSpec((None, 8, R), lambda g: (g, 0, 0))
    stats0 = pl.pallas_call(
        functools.partial(near_stats, n=n, d=d, cut=cut, c2=c2),
        grid=(kv,),
        in_specs=[rows_blk, rows_blk, own_blk],
        out_specs=stat_blk,
        out_shape=jax.ShapeDtypeStruct((kv, 8, R), F32),
        cost_estimate=cost(2_500_000_000, 6_000_000),
        name="near_stats",
    )(q4, do4, own)

    buf_b, *arr_a = lax.optimization_barrier((buf_b, *arr_a))
    arr_b = []
    for h in range(1, HOPS + 1):
        arr_b.append(shift(buf_b, h))

    def call(head, arrived, extra):
        blk = pl.BlockSpec((n, None, group, d), lambda c, *s: (0, head, 0, 0))
        st = pl.BlockSpec((None, 8, R), lambda c, *s: (head, 0, 0))
        turn_spec = pl.BlockSpec((2 * d, d), lambda c, *s: (n // d, 0))
        row_spec = pl.BlockSpec((2 * n, d), lambda c, *s: (0, 0))
        in_specs = [blk, blk] + [row_spec] * HOPS + [turn_spec] * HOPS + [st]
        args = [q4, do4, *arrived, *arr_a, stats0]
        alias = {}
        dms = [jax.ShapeDtypeStruct((d, d), BF16)] * HOPS
        if head:
            prev_dq, prev_st, prev_dm = extra
            in_specs += [whole(prev_dm.shape)] + [pl.BlockSpec(memory_space=pl.ANY)] * 2
            args += [prev_dm, prev_dq, prev_st]
            alias = {len(args): 0, len(args) + 1: 1}
        else:
            dms = [jax.ShapeDtypeStruct((HOPS, d, d), F32)]
        yshape = jax.ShapeDtypeStruct((2 * n, d), BF16)
        return pl.pallas_call(
            functools.partial(
                far,
                head=head, n=n, d=d, hops=HOPS, c2=c2, factor=factor, blocks=blocks,
            ),
            grid_spec=pltpu.PrefetchScalarGridSpec(
                num_scalar_prefetch=2,
                grid=(1,),
                in_specs=in_specs,
                out_specs=[pl.BlockSpec((None, d, R), lambda c, *s: (head, 0, 0)), st]
                + [whole((2 * n, d))] * HOPS
                + [whole(x.shape) for x in dms],
                scratch_shapes=[
                    pltpu.VMEM((HOPS, d, d), F32),
                    pltpu.VMEM((HOPS, n, d), BF16),
                    pltpu.VMEM((HOPS, n, d), BF16),
                    pltpu.VMEM((HOPS, d, n), BF16),
                    pltpu.VMEM((HOPS, n, d), F32),
                    pltpu.VMEM((HOPS, n, d), F32),
                    pltpu.VMEM((HOPS, n, R), F32),
                    pltpu.VMEM((HOPS, n, R), F32),
                    pltpu.VMEM((HOPS, 1, R), F32),
                ],
            ),
            out_shape=[
                jax.ShapeDtypeStruct((kv, d, R), F32),
                jax.ShapeDtypeStruct((kv, 8, R), F32),
                yshape, yshape, yshape, *dms,
            ],
            input_output_aliases=alias,
            compiler_params=pltpu.CompilerParams(vmem_limit_bytes=56 << 20),
            cost_estimate=cost(9_000_000_000, 6_000_000),
        )(window, first_block, *args)

    dq, st, *ys_a, dm_a = call(0, arr_a, None)
    back_a = []
    for h in range(HOPS):
        back_a.append(shift(ys_a[h], -h - 1))
    dq, st, y1, y2, y3, *dms = call(1, arr_b, (dq, st, dm_a))
    dt, back_b = [], []
    for h in range(HOPS):
        dt.append(shift(dms[h], -h - 1))
    for h, y in enumerate((y1, y2, y3)):
        back_b.append(shift(y, -h - 1))

    dq_out, own_grad = pl.pallas_call(
        functools.partial(near, n=n, d=d, cut=cut, c2=c2, factor=factor),
        grid=(kv,),
        in_specs=[rows_blk, rows_blk, own_blk, stat_blk, pl.BlockSpec((None, d, R), lambda g: (g, 0, 0))],
        out_specs=[rows_blk, own_blk],
        out_shape=[
            jax.ShapeDtypeStruct((n, kv, group, d), BF16),
            jax.ShapeDtypeStruct((kv, 2 * n, d), F32),
        ],
        cost_estimate=cost(5_000_000_000, 9_000_000),
        name="near",
    )(q4, do4, own, st, dq)

    turn = dt[0].astype(F32) + dt[1].astype(F32) + dt[2].astype(F32)
    peers = lax.axis_size("kv")
    half = turn.astype(BF16)
    total = turn
    for k in range(1, peers):
        sent = lax.ppermute(half, "kv", [(i, (i + k) % peers) for i in range(peers)])
        total = total + sent.astype(F32)

    key_grad, value_grad = pl.pallas_call(
        functools.partial(finish, n=n),
        out_shape=[jax.ShapeDtypeStruct((2 * n, d), BF16)] * 2,
        scratch_shapes=[pltpu.VMEM((2 * n, d), F32)],
        name="finish",
    )(own_grad, *back_a, *back_b)
    return (
        dq_out.reshape(n, heads, d),
        key_grad.reshape(n, kv, d),
        value_grad.reshape(n, kv, d),
        total[None],
    )


def solution(mesh):
    return jax.shard_map(
        shards,
        mesh=mesh,
        in_specs=(
            P("ctx", "kv", None),
            P("ctx", "kv", None),
            P("ctx", "kv", None),
            P("ctx", "kv", None),
            P("ctx", None, None),
            P("kv"),
            P(),
        ),
        out_specs=(
            P("ctx", "kv", None),
            P("ctx", "kv", None),
            P("ctx", "kv", None),
            P("ctx", None, None),
        ),
        check_vma=False,
    )
```

profile of v0, /device:TPU:14, one launch (start us, length us, event | category | flops | bytes accessed | tf_op | source)
XLA Modules:
  0.0 119.2 jit_solution(2197437819169098044)
XLA Ops:
  0.6 2.0 %prepare.1 = (bf16[1024,128]{1,0:T(8,128)(2,1)}, bf16[768,128]{1,0:T(8,128)(2,1)}, bf16[2,768,128]{2,1,0:T(8,128)(2,1)}) custom-call(bf16[768,128]{1,0:T(8,128)(2,1)} %bitcast.10, bf16[768,128]{1,0:T(8,128)(2,1)} %bitcast.11, f32[128,128]{1,0:T(8,128)} %bitcast.12), custom_call_target="tpu_custom_call" | custom-call | tf_op jit(solution)/shard_map/prepare/pallas_call | solution.py:218
  2.7 3.7 %collective-permute-start.2 = (bf16[1024,128]{1,0:T(8,128)(2,1)}, bf16[1024,128]{1,0:T(8,128)(2,1)S(1)}, u32[]{:S(2)}, u32[]{:S(2)}) collective-permute-start(bf16[1024,128]{1,0:T(8,128)(2,1)} %get-tuple-element.31), channel_id=1, source_target_pairs={{0,12},{4,16},{8,20},{12,24},{16,28},{20,32},{24,36},{28,40},{32,4... | collective-permute-start | bytes 786440 | tf_op jit(solution)/shard_map/ppermute | solution.py:34
  6.3 2.6 %collective-permute-start.1 = (bf16[1024,128]{1,0:T(8,128)(2,1)}, bf16[1024,128]{1,0:T(8,128)(2,1)S(1)}, u32[]{:S(2)}, u32[]{:S(2)}) collective-permute-start(bf16[1024,128]{1,0:T(8,128)(2,1)} %get-tuple-element.31), channel_id=1, source_target_pairs={{0,8},{4,12},{8,16},{12,20},{16,24},{20,28},{24,32},{28,36},{32,40... | collective-permute-start | bytes 786440 | tf_op jit(solution)/shard_map/ppermute | solution.py:34
  8.9 1.9 %collective-permute-start = (bf16[1024,128]{1,0:T(8,128)(2,1)}, bf16[1024,128]{1,0:T(8,128)(2,1)S(1)}, u32[]{:S(2)}, u32[]{:S(2)}) collective-permute-start(bf16[1024,128]{1,0:T(8,128)(2,1)} %get-tuple-element.31), channel_id=1, source_target_pairs={{0,4},{4,8},{8,12},{12,16},{16,20},{20,24},{24,28},{28,32},{32,36}... | collective-permute-start | bytes 786440 | tf_op jit(solution)/shard_map/ppermute | solution.py:34
  11.5 4.5 %near_stats.1.near_ref = f32[2,8,3072]{2,1,0:T(8,128)} custom-call(bf16[384,2,8,128]{3,2,1,0:T(8,128)(2,1)} %bitcast.13, bf16[384,2,8,128]{3,2,1,0:T(8,128)(2,1)} %bitcast.17, bf16[2,768,128]{2,1,0:T(8,128)(2,1)} %get-tuple-element.29.own_ref), custom_call_target="tpu_custom_call" | custom-call | flops 2500000000 | bytes 6000000 | tf_op jit(solution)/shard_map/near_stats/pallas_call | solution.py:236
  16.0 3.6 %collective-permute-done.1.r2_ref.t2_ref = bf16[1024,128]{1,0:T(8,128)(2,1)S(1)} collective-permute-done((bf16[1024,128]{1,0:T(8,128)(2,1)}, bf16[1024,128]{1,0:T(8,128)(2,1)S(1)}, u32[]{:S(2)}, u32[]{:S(2)}) %collective-permute-start.1) | collective-permute-done | bytes 262176 | tf_op jit(solution)/shard_map/ppermute | solution.py:34
  19.6 2.0 %collective-permute-done.r1_ref.t1_ref = bf16[1024,128]{1,0:T(8,128)(2,1)S(1)} collective-permute-done((bf16[1024,128]{1,0:T(8,128)(2,1)}, bf16[1024,128]{1,0:T(8,128)(2,1)S(1)}, u32[]{:S(2)}, u32[]{:S(2)}) %collective-permute-start) | collective-permute-done | bytes 262176 | tf_op jit(solution)/shard_map/ppermute | solution.py:34
  21.6 10.9 %collective-permute-start.5 = (bf16[768,128]{1,0:T(8,128)(2,1)S(1)}, bf16[768,128]{1,0:T(8,128)(2,1)S(1)}, u32[]{:S(2)}, u32[]{:S(2)}) collective-permute-start(bf16[768,128]{1,0:T(8,128)(2,1)S(1)} %copy-done.15), channel_id=1, source_target_pairs={{0,12},{4,16},{8,20},{12,24},{16,28},{20,32},{24,36},{28,40},{32,4... | collective-permute-start | bytes 589832 | tf_op jit(solution)/shard_map/ppermute | solution.py:34
  32.5 1.5 %collective-permute-start.3 = (bf16[768,128]{1,0:T(8,128)(2,1)S(1)}, bf16[768,128]{1,0:T(8,128)(2,1)S(1)}, u32[]{:S(2)}, u32[]{:S(2)}) collective-permute-start(bf16[768,128]{1,0:T(8,128)(2,1)S(1)} %copy-done.15), channel_id=1, source_target_pairs={{0,4},{4,8},{8,12},{12,16},{16,20},{20,24},{24,28},{28,32},{32,36}... | collective-permute-start | bytes 589832 | tf_op jit(solution)/shard_map/ppermute | solution.py:34
  34.0 11.6 %shard_map.102 = (f32[2,128,3072]{2,1,0:T(8,128)}, f32[2,8,3072]{2,1,0:T(8,128)}, bf16[768,128]{1,0:T(8,128)(2,1)}, bf16[768,128]{1,0:T(8,128)(2,1)}, bf16[768,128]{1,0:T(8,128)(2,1)}, /*index=5*/f32[3,128,128]{2,1,0:T(8,128)}) custom-call(s32[2]{0:T(128)} %win.3, s32[1]{0:T(128)S(6)} %copy.15.fst, bf16[384,2,8,128]{3,2,1,0:T(8,128)(2,1)} %bitcast.14, ...), custom_call_target="tpu_custom_call" | custom-call | flops 8999999488 | bytes 6000000 | tf_op jit(solution)/shard_map/pallas_call | solution.py:268
  45.7 0.6 copy-done.16
  46.5 9.6 %shard_map.103 = (f32[2,128,3072]{2,1,0:T(8,128)}, f32[2,8,3072]{2,1,0:T(8,128)}, bf16[768,128]{1,0:T(8,128)(2,1)}, bf16[768,128]{1,0:T(8,128)(2,1)}, bf16[768,1...) custom-call(s32[2]{0:T(128)} %win.3, ...), custom_call_target="tpu_custom_call", output_to_operand_aliasing={{0}: (12, {}), {1}: (13, {})} | custom-call | flops 8999999488 | bytes 6000000 | tf_op jit(solution)/shard_map/pallas_call | solution.py:268
  56.7 4.4 %collective-permute-start.13 = (bf16[128,128]{1,0:T(8,128)(2,1)}, bf16[128,128]{1,0:T(8,128)(2,1)S(1)}, u32[]{:S(2)}, u32[]{:S(2)}) collective-permute-start(bf16[128,128]{1,0:T(8,128)(2,1)} %get-tuple-element.52), channel_id=1, source_target_pairs={{0,120},{4,124},{8,0},{12,4},{16,8},{20,12},{24,16},{28,20},{32,24... | collective-permute-start | bytes 98312 | tf_op jit(solution)/shard_map/ppermute | solution.py:34
  61.1 0.7 collective-permute-start.6
  61.8 1.2 %collective-permute-done.13 = bf16[128,128]{1,0:T(8,128)(2,1)S(1)} collective-permute-done((bf16[128,128]{1,0:T(8,128)(2,1)}, bf16[128,128]{1,0:T(8,128)(2,1)S(1)}, u32[]{:S(2)}, u32[]{:S(2)}) %collective-permute-start.13) | collective-permute-done | bytes 32800 | tf_op jit(solution)/shard_map/ppermute | solution.py:34
  63.0 7.1 %collective-permute-done.14 = bf16[128,128]{1,0:T(8,128)(2,1)S(1)} collective-permute-done((bf16[128,128]{1,0:T(8,128)(2,1)}, bf16[128,128]{1,0:T(8,128)(2,1)S(1)}, u32[]{:S(2)}, u32[]{:S(2)}) %collective-permute-start.14) | collective-permute-done | bytes 32800 | tf_op jit(solution)/shard_map/ppermute | solution.py:34
  70.2 11.1 %collective-permute-start.16 = (bf16[128,128]{1,0:T(8,128)(2,1)S(1)}, bf16[128,128]{1,0:T(8,128)(2,1)S(1)}, u32[]{:S(2)}, u32[]{:S(2)}) collective-permute-start(bf16[128,128]{1,0:T(8,128)(2,1)S(1)} %fusion), channel_id=1, source_target_pairs={{0,2},{1,3},{2,0},{3,1},{4,6},{5,7},{6,4},{7,5},{8,10},{9,11},{10,... | collective-permute-start | bytes 98312 | tf_op jit(solution)/shard_map/ppermute | solution.py:331
  81.4 7.5 %near.1 = (bf16[384,2,8,128]{3,2,1,0:T(8,128)(2,1)}, f32[2,768,128]{2,1,0:T(8,128)}) custom-call(bf16[384,2,8,128]{3,2,1,0:T(8,128)(2,1)} %bitcast.16, bf16[384,2,8,128]{3,2,1,0:T(8,128)(2,1)} %bitcast.20, bf16[2,768,128]{2,1,0:T(8,128)(2,1)} %get-tuple-element.29.own_ref, f32[2,8,3072]{2,1,0:T(8,128)} %get-tuple-element.39.stat_ref, ...), custom_call_target="tpu_custom_call" | custom-call | flops 5000000000 | bytes 9000000 | tf_op jit(solution)/shard_map/near/pallas_call | solution.py:313
  89.2 3.0 %collective-permute-start.11 = (bf16[768,128]{1,0:T(8,128)(2,1)S(1)}, bf16[768,128]{1,0:T(8,128)(2,1)S(1)}, u32[]{:S(2)}, u32[]{:S(2)}) collective-permute-start(bf16[768,128]{1,0:T(8,128)(2,1)S(1)} %copy-done.11), channel_id=1, source_target_pairs={{0,116},{4,120},{8,124},{12,0},{16,4},{20,8},{24,12},{28,16},{32,2... | collective-permute-start | bytes 589832 | tf_op jit(solution)/shard_map/ppermute | solution.py:34
  92.2 0.7 add_bitcast_fusion
  92.9 8.4 %collective-permute-done.8.refs_2_ = bf16[768,128]{1,0:T(8,128)(2,1)S(1)} collective-permute-done((bf16[768,128]{1,0:T(8,128)(2,1)S(1)}, bf16[768,128]{1,0:T(8,128)(2,1)S(1)}, u32[]{:S(2)}, u32[]{:S(2)}) %collective-permute-start.8) | collective-permute-done | bytes 196640 | tf_op jit(solution)/shard_map/ppermute | solution.py:34
  101.3 14.8 %collective-permute-done.11.refs_5_ = bf16[768,128]{1,0:T(8,128)(2,1)S(1)} collective-permute-done((bf16[768,128]{1,0:T(8,128)(2,1)S(1)}, bf16[768,128]{1,0:T(8,128)(2,1)S(1)}, u32[]{:S(2)}, u32[]{:S(2)}) %collective-permute-start.11) | collective-permute-done | bytes 196640 | tf_op jit(solution)/shard_map/ppermute | solution.py:34
  116.1 0.6 copy-done.5
  116.8 2.5 %finish.1 = (bf16[768,128]{1,0:T(8,128)(2,1)}, bf16[768,128]{1,0:T(8,128)(2,1)}) custom-call(f32[2,768,128]{2,1,0:T(8,128)} %get-tuple-element.42.own_ref, bf16[768,128]{1,0:T(8,128)(2,1)} %copy-done, bf16[768,128]{1,0:T(8,128)(2,1)} %copy-done.1, bf16[768,128]{1,0:T(8,128)(2,1)} %copy-done.2, bf16[768,128]{1,0:T(8,128)(2,1)} %copy-done.3, ...), custom_call_target="tpu_custom_call" | custom-call | tf_op jit(solution)/shard_map/finish/pallas_call | solution.py:334
  (58 shorter events, 1.2 us)
Async XLA Ops:
  2.7 13.3 %collective-permute-start.2 = (bf16[1024,128]{1,0:T(8,128)(2,1)}, bf16[1024,128]{1,0:T(8,128)(2,1)S(1)}, u32[]{:S(2)}, u32[]{:S(2)}) collective-permute-start(bf16[1024,128]{1,0:T(8,128)(2,1)} %get-tuple-element.31), channel_id=1, source_target_pairs={{0,12},{4,16},{8,20},{12,24},{16,28},{20,32},{24,36},{28,40},{32,4... | collective-permute-start | bytes 786440 | tf_op jit(solution)/shard_map/ppermute | solution.py:34
  6.3 13.2 %collective-permute-start.1 = (bf16[1024,128]{1,0:T(8,128)(2,1)}, bf16[1024,128]{1,0:T(8,128)(2,1)S(1)}, u32[]{:S(2)}, u32[]{:S(2)}) collective-permute-start(bf16[1024,128]{1,0:T(8,128)(2,1)} %get-tuple-element.31), channel_id=1, source_target_pairs={{0,8},{4,12},{8,16},{12,20},{16,24},{20,28},{24,32},{28,36},{32,40... | collective-permute-start | bytes 786440 | tf_op jit(solution)/shard_map/ppermute | solution.py:34
  8.9 12.7 %collective-permute-start = (bf16[1024,128]{1,0:T(8,128)(2,1)}, bf16[1024,128]{1,0:T(8,128)(2,1)S(1)}, u32[]{:S(2)}, u32[]{:S(2)}) collective-permute-start(bf16[1024,128]{1,0:T(8,128)(2,1)} %get-tuple-element.31), channel_id=1, source_target_pairs={{0,4},{4,8},{8,12},{12,16},{16,20},{20,24},{24,28},{28,32},{32,36}... | collective-permute-start | bytes 786440 | tf_op jit(solution)/shard_map/ppermute | solution.py:34
  15.9 18.1 %copy-start.6 = (bf16[1024,128]{1,0:T(8,128)(2,1)}, bf16[1024,128]{1,0:T(8,128)(2,1)S(1)}, u32[]{:S(2)}) copy-start(bf16[1024,128]{1,0:T(8,128)(2,1)S(1)} %collective-permute-done.2.r3_ref.t3_ref) | copy-start | bytes 786436
  21.6 24.1 %collective-permute-start.5 = (bf16[768,128]{1,0:T(8,128)(2,1)S(1)}, bf16[768,128]{1,0:T(8,128)(2,1)S(1)}, u32[]{:S(2)}, u32[]{:S(2)}) collective-permute-start(bf16[768,128]{1,0:T(8,128)(2,1)S(1)} %copy-done.15), channel_id=1, source_target_pairs={{0,12},{4,16},{8,20},{12,24},{16,28},{20,32},{24,36},{28,40},{32,4... | collective-permute-start | bytes 589832 | tf_op jit(solution)/shard_map/ppermute | solution.py:34
  32.5 13.2 %collective-permute-start.4 = (bf16[768,128]{1,0:T(8,128)(2,1)S(1)}, bf16[768,128]{1,0:T(8,128)(2,1)S(1)}, u32[]{:S(2)}, u32[]{:S(2)}) collective-permute-start(bf16[768,128]{1,0:T(8,128)(2,1)S(1)} %copy-done.15), channel_id=1, source_target_pairs={{0,8},{4,12},{8,16},{12,20},{16,24},{20,28},{24,32},{28,36},{32,40... | collective-permute-start | bytes 589832 | tf_op jit(solution)/shard_map/ppermute | solution.py:34
  32.5 13.2 %collective-permute-start.3 = (bf16[768,128]{1,0:T(8,128)(2,1)S(1)}, bf16[768,128]{1,0:T(8,128)(2,1)S(1)}, u32[]{:S(2)}, u32[]{:S(2)}) collective-permute-start(bf16[768,128]{1,0:T(8,128)(2,1)S(1)} %copy-done.15), channel_id=1, source_target_pairs={{0,4},{4,8},{8,12},{12,16},{16,20},{20,24},{24,28},{28,32},{32,36}... | collective-permute-start | bytes 589832 | tf_op jit(solution)/shard_map/ppermute | solution.py:34
  46.5 15.3 %copy-start.10 = (bf16[768,128]{1,0:T(8,128)(2,1)S(1)}, bf16[768,128]{1,0:T(8,128)(2,1)}, u32[]{:S(2)}) copy-start(bf16[768,128]{1,0:T(8,128)(2,1)} %get-tuple-element.44) | copy-start | bytes 589828
  56.1 5.6 %collective-permute-start.12 = (bf16[128,128]{1,0:T(8,128)(2,1)}, bf16[128,128]{1,0:T(8,128)(2,1)S(1)}, u32[]{:S(2)}, u32[]{:S(2)}) collective-permute-start(bf16[128,128]{1,0:T(8,128)(2,1)} %get-tuple-element.51), channel_id=1, source_target_pairs={{0,124},{4,0},{8,4},{12,8},{16,12},{20,16},{24,20},{28,24},{32,28}... | collective-permute-start | bytes 98312 | tf_op jit(solution)/shard_map/ppermute | solution.py:34
  56.7 6.3 %collective-permute-start.13 = (bf16[128,128]{1,0:T(8,128)(2,1)}, bf16[128,128]{1,0:T(8,128)(2,1)S(1)}, u32[]{:S(2)}, u32[]{:S(2)}) collective-permute-start(bf16[128,128]{1,0:T(8,128)(2,1)} %get-tuple-element.52), channel_id=1, source_target_pairs={{0,120},{4,124},{8,0},{12,4},{16,8},{20,12},{24,16},{28,20},{32,24... | collective-permute-start | bytes 98312 | tf_op jit(solution)/shard_map/ppermute | solution.py:34
  61.1 9.0 %collective-permute-start.14 = (bf16[128,128]{1,0:T(8,128)(2,1)}, bf16[128,128]{1,0:T(8,128)(2,1)S(1)}, u32[]{:S(2)}, u32[]{:S(2)}) collective-permute-start(bf16[128,128]{1,0:T(8,128)(2,1)} %get-tuple-element.53), channel_id=1, source_target_pairs={{0,116},{4,120},{8,124},{12,0},{16,4},{20,8},{24,12},{28,16},{32,2... | collective-permute-start | bytes 98312 | tf_op jit(solution)/shard_map/ppermute | solution.py:34
  61.1 27.8 %collective-permute-start.6 = (bf16[768,128]{1,0:T(8,128)(2,1)S(1)}, bf16[768,128]{1,0:T(8,128)(2,1)S(1)}, u32[]{:S(2)}, u32[]{:S(2)}) collective-permute-start(bf16[768,128]{1,0:T(8,128)(2,1)S(1)} %copy-done.14), channel_id=1, source_target_pairs={{0,124},{4,0},{8,4},{12,8},{16,12},{20,16},{24,20},{28,24},{32,28}... | collective-permute-start | bytes 589832 | tf_op jit(solution)/shard_map/ppermute | solution.py:34
  61.8 31.1 %collective-permute-start.7 = (bf16[768,128]{1,0:T(8,128)(2,1)S(1)}, bf16[768,128]{1,0:T(8,128)(2,1)S(1)}, u32[]{:S(2)}, u32[]{:S(2)}) collective-permute-start(bf16[768,128]{1,0:T(8,128)(2,1)S(1)} %copy-done.10), channel_id=1, source_target_pairs={{0,120},{4,124},{8,0},{12,4},{16,8},{20,12},{24,16},{28,20},{32,24... | collective-permute-start | bytes 589832 | tf_op jit(solution)/shard_map/ppermute | solution.py:34
  70.1 18.9 %collective-permute-start.17 = (bf16[128,128]{1,0:T(8,128)(2,1)S(1)}, bf16[128,128]{1,0:T(8,128)(2,1)S(1)}, u32[]{:S(2)}, u32[]{:S(2)}) collective-permute-start(bf16[128,128]{1,0:T(8,128)(2,1)S(1)} %fusion), channel_id=1, source_target_pairs={{0,3},{1,0},{2,1},{3,2},{4,7},{5,4},{6,5},{7,6},{8,11},{9,8},{10,9... | collective-permute-start | bytes 98312 | tf_op jit(solution)/shard_map/ppermute | solution.py:331
  70.2 18.9 %collective-permute-start.16 = (bf16[128,128]{1,0:T(8,128)(2,1)S(1)}, bf16[128,128]{1,0:T(8,128)(2,1)S(1)}, u32[]{:S(2)}, u32[]{:S(2)}) collective-permute-start(bf16[128,128]{1,0:T(8,128)(2,1)S(1)} %fusion), channel_id=1, source_target_pairs={{0,2},{1,3},{2,0},{3,1},{4,6},{5,7},{6,4},{7,5},{8,10},{9,11},{10,... | collective-permute-start | bytes 98312 | tf_op jit(solution)/shard_map/ppermute | solution.py:331
  81.3 7.9 %collective-permute-start.15 = (bf16[128,128]{1,0:T(8,128)(2,1)S(1)}, bf16[128,128]{1,0:T(8,128)(2,1)S(1)}, u32[]{:S(2)}, u32[]{:S(2)}) collective-permute-start(bf16[128,128]{1,0:T(8,128)(2,1)S(1)} %fusion), channel_id=1, source_target_pairs={{0,1},{1,2},{2,3},{3,0},{4,5},{5,6},{6,7},{7,4},{8,9},{9,10},{10,1... | collective-permute-start | bytes 98312 | tf_op jit(solution)/shard_map/ppermute | solution.py:331
  88.9 27.2 %copy-start = (bf16[768,128]{1,0:T(8,128)(2,1)}, bf16[768,128]{1,0:T(8,128)(2,1)S(1)}, u32[]{:S(2)}) copy-start(bf16[768,128]{1,0:T(8,128)(2,1)S(1)} %collective-permute-done.6.refs_0_) | copy-start | bytes 589828
  88.9 12.4 %collective-permute-start.8 = (bf16[768,128]{1,0:T(8,128)(2,1)S(1)}, bf16[768,128]{1,0:T(8,128)(2,1)S(1)}, u32[]{:S(2)}, u32[]{:S(2)}) collective-permute-start(bf16[768,128]{1,0:T(8,128)(2,1)S(1)} %copy-done.9), channel_id=1, source_target_pairs={{0,116},{4,120},{8,124},{12,0},{16,4},{20,8},{24,12},{28,16},{32,2... | collective-permute-start | bytes 589832 | tf_op jit(solution)/shard_map/ppermute | solution.py:34
  89.0 12.3 %collective-permute-start.9 = (bf16[768,128]{1,0:T(8,128)(2,1)S(1)}, bf16[768,128]{1,0:T(8,128)(2,1)S(1)}, u32[]{:S(2)}, u32[]{:S(2)}) collective-permute-start(bf16[768,128]{1,0:T(8,128)(2,1)S(1)} %copy-done.13), channel_id=1, source_target_pairs={{0,124},{4,0},{8,4},{12,8},{16,12},{20,16},{24,20},{28,24},{32,28}... | collective-permute-start | bytes 589832 | tf_op jit(solution)/shard_map/ppermute | solution.py:34
  89.1 12.2 %collective-permute-start.10 = (bf16[768,128]{1,0:T(8,128)(2,1)S(1)}, bf16[768,128]{1,0:T(8,128)(2,1)S(1)}, u32[]{:S(2)}, u32[]{:S(2)}) collective-permute-start(bf16[768,128]{1,0:T(8,128)(2,1)S(1)} %copy-done.12), channel_id=1, source_target_pairs={{0,120},{4,124},{8,0},{12,4},{16,8},{20,12},{24,16},{28,20},{32,24... | collective-permute-start | bytes 589832 | tf_op jit(solution)/shard_map/ppermute | solution.py:34
  89.2 26.9 %collective-permute-start.11 = (bf16[768,128]{1,0:T(8,128)(2,1)S(1)}, bf16[768,128]{1,0:T(8,128)(2,1)S(1)}, u32[]{:S(2)}, u32[]{:S(2)}) collective-permute-start(bf16[768,128]{1,0:T(8,128)(2,1)S(1)} %copy-done.11), channel_id=1, source_target_pairs={{0,116},{4,120},{8,124},{12,0},{16,4},{20,8},{24,12},{28,16},{32,2... | collective-permute-start | bytes 589832 | tf_op jit(solution)/shard_map/ppermute | solution.py:34
  92.9 23.2 %copy-start.1 = (bf16[768,128]{1,0:T(8,128)(2,1)}, bf16[768,128]{1,0:T(8,128)(2,1)S(1)}, u32[]{:S(2)}) copy-start(bf16[768,128]{1,0:T(8,128)(2,1)S(1)} %collective-permute-done.7.refs_1_) | copy-start | bytes 589828
  101.3 14.9 %copy-start.3 = (bf16[768,128]{1,0:T(8,128)(2,1)}, bf16[768,128]{1,0:T(8,128)(2,1)S(1)}, u32[]{:S(2)}) copy-start(bf16[768,128]{1,0:T(8,128)(2,1)S(1)} %collective-permute-done.9.refs_3_) | copy-start | bytes 589828
  101.3 14.9 %copy-start.4 = (bf16[768,128]{1,0:T(8,128)(2,1)}, bf16[768,128]{1,0:T(8,128)(2,1)S(1)}, u32[]{:S(2)}) copy-start(bf16[768,128]{1,0:T(8,128)(2,1)S(1)} %collective-permute-done.10.refs_4_) | copy-start | bytes 589828
  (13 other events, 99.9 us)
where the time goes:
time: 120 us; the launch traced here: 119 us
  starting transfers between devices  40.7 us (34%)
  Pallas kernels  37.7 us (31%)
  waiting for transfers between devices  37.2 us (31%)
  between operations  1.49 us (1%)
  local copies, waits for them, and re-layouts  1.46 us (1%)
    ppermute x15, waiting for transfers between devices, shift(): return lax.ppermute(x, 'ctx', [(i, (i + by) % n) for i in range(n)])  37.2 us
    ppermute x15, starting transfers between devices, shift(): return lax.ppermute(x, 'ctx', [(i, (i + by) % n) for i in range(n)])  29.4 us
    pallas_call x2, Pallas kernels, call(): pl.pallas_call(functools.partial(far, head=head, n=n, d=d, hops=HOPS, c2=...  21.3 us
    ppermute x3, starting transfers between devices, shards(): lax.ppermute(half, 'kv', [(i, (i + k) % peers) for i in range(peers)])  11.3 us
    pallas_call x1, Pallas kernels, shards(): pl.pallas_call(functools.partial(near, n=n, d=d, cut=cut, c2=c2, factor=f...  7.46 us
    pallas_call x1, Pallas kernels, shards(): pl.pallas_call(functools.partial(near_stats, n=n, d=d, cut=cut, c2=c2), g...  4.46 us
    pallas_call x1, Pallas kernels, shards(): pl.pallas_call(functools.partial(finish, n=n), out_shape=[jax.ShapeDtypeS...  2.48 us
  transfers between devices with their start and end apart: 18, of which 6 were waited for; matrix products, arithmetic and copies ran while one was open for 1% of the time, Pallas kernels for 20%

commit v1 on v0

--- a/solution.py
+++ b/solution.py
@@ -18,15 +18,14 @@
     return lax.dot_general(a, b, (((ca,), (cb,)), ((), ())), preferred_element_type=F32)
 
 
-def dot_precise(a, b, ca, cb):
-    return lax.dot_general(
-        a, b, (((ca,), (cb,)), ((), ())), preferred_element_type=F32, precision=lax.Precision.HIGHEST
-    )
-
-
 def halves(x):
     upper = x.astype(BF16)
     return upper, (x - upper.astype(F32)).astype(BF16)
+
+
+def dot_split(a, b, ca, cb):
+    upper, lower = halves(a)
+    return dot(upper, b, ca, cb) + dot(lower, b, ca, cb)
 
 
 def shift(x, by):
@@ -42,9 +41,7 @@
             rows = wide[pl.ds(g, n, stride=2)].astype(BF16)
             out[part * n : (part + 1) * n] = rows
             own_ref[g, part * n : (part + 1) * n] = rows
-    upper, lower = halves(t_ref[...])
-    a_ref[2 * n : 2 * n + d] = upper
-    a_ref[2 * n + d : 2 * n + 2 * d] = lower
+    a_ref[2 * n : 2 * n + d] = t_ref[...].astype(BF16)
 
 
 def diagonal(s, first, group):
@@ -76,34 +73,45 @@
     if head:
         prev_dm, rest = rest[0], rest[3:]
     dq_ref, stat_ref, y1_ref, y2_ref, y3_ref = rest[0:5]
-    dm_refs = rest[5:-9]
-    prod, keys, vals, keys_t, dk, dv, e_ref, p_ref, tops = rest[-9:]
-    group = q_ref.shape[1]
+    dm_refs = rest[5:-12]
+    prod, keys, vals, keys_t, dk, dv, e_ref, p_ref, tops, q_buf, do_buf, sems = rest[-12:]
+    group = q_ref.shape[2]
     R = n * group
     place = lax.rem(lax.axis_index("ctx") - fst[0] + blocks, blocks)
     live = jnp.minimum(win[head], place + 1) - 1
     sources = (r1_ref, r2_ref, r3_ref)
     turns = (t1_ref, t2_ref, t3_ref)
 
+    copies = [
+        pltpu.make_async_copy(src.at[:, head], dst, sems.at[k])
+        for k, (src, dst) in enumerate(((q_ref, q_buf), (do_ref, do_buf)))
+    ]
+    for copy in copies:
+        copy.start()
     dk[...] = jnp.zeros_like(dk)
     dv[...] = jnp.zeros_like(dv)
     total = None
     for i in range(hops):
-        mat = turns[i][0:d].astype(F32) + turns[i][d : 2 * d].astype(F32)
-        total = mat if total is None else dot_precise(total, mat, 1, 0)
-        prod[i] = total
+        mat = turns[i][...]
+        total = mat.astype(F32) if total is None else dot_split(total, mat, 1, 0)
         upper, lower = halves(total)
+        prod[i] = upper
         raw = sources[i][0:n]
-        tile = (dot(raw, upper, 1, 1) + dot(raw, lower, 1, 1)).astype(BF16)
+        tile = dot(raw, upper, 1, 1)
+        if i:
+            tile = tile + dot(raw, lower, 1, 1)
+        tile = tile.astype(BF16)
         keys[i] = tile
         keys_t[i] = tile.T
         vals[i] = sources[i][n : 2 * n]
     stat_ref[...] = near_ref[...]
     dq_ref[...] = jnp.zeros_like(dq_ref)
+    for copy in copies:
+        copy.wait()
 
     def forward(i, carry):
-        q = q_ref[...].reshape(R, d)
-        do = do_ref[...].reshape(R, d)
+        q = q_buf[...].reshape(R, d)
+        do = do_buf[...].reshape(R, d)
         s = dot(keys[i], q, 1, 1)
         dp = dot(vals[i], do, 1, 1)
         m = stat_ref[0:1]
@@ -124,8 +132,8 @@
     stat_ref[2:3] = stat_ref[2:3] * inv
 
     def backward(i, carry):
-        q = q_ref[...].reshape(R, d)
-        do = do_ref[...].reshape(R, d)
+        q = q_buf[...].reshape(R, d)
+        do = do_buf[...].reshape(R, d)
         w = e_ref[i] * (jnp.exp2((tops[i] - stat_ref[0:1]) * c2) * stat_ref[1:2])
         ds = (w * (p_ref[i] - stat_ref[2:3])).astype(BF16)
         dv[i] = dot(w.astype(BF16), do, 1, 0)
@@ -137,20 +145,16 @@
 
     grads = []
     for i, y_ref in enumerate((y1_ref, y2_ref, y3_ref)):
-        g_up, g_lo = halves(dk[i] * factor)
-        p_up, p_lo = halves(prod[i])
-        back = dot(g_up, p_up, 1, 0) + dot(g_up, p_lo, 1, 0) + dot(g_lo, p_up, 1, 0)
-        y_ref[0:n] = back.astype(BF16)
+        g = (dk[i] * factor).astype(BF16)
+        y_ref[0:n] = dot(g, prod[i], 1, 0).astype(BF16)
         y_ref[n : 2 * n] = dv[i].astype(BF16)
-        raw = sources[i][0:n]
-        grads.append(dot(g_up, raw, 0, 0) + dot(g_lo, raw, 0, 0))
+        grads.append(dot(g, sources[i][0:n], 0, 0))
     if head:
-        t2, t3 = [t[0:d].astype(F32) + t[d : 2 * d].astype(F32) for t in turns[1:]]
         dm1, dm2, dm3 = [grads[i] + prev_dm[i] for i in range(3)]
-        mid = dm2 + dot_precise(dm3, t3, 1, 1)
-        dm_refs[0][...] = (dm1 + dot_precise(mid, t2, 1, 1)).astype(BF16)
-        dm_refs[1][...] = dot_precise(prod[0], mid, 0, 0).astype(BF16)
-        dm_refs[2][...] = dot_precise(prod[1], dm3, 0, 0).astype(BF16)
+        mid = dm2 + dot_split(dm3, turns[2][...], 1, 1)
+        y1_ref[2 * n : 2 * n + d] = (dm1 + dot_split(mid, turns[1][...], 1, 1)).astype(BF16)
+        y2_ref[2 * n : 2 * n + d] = dot(turns[0][...], mid.astype(BF16), 0, 0).astype(BF16)
+        y3_ref[2 * n : 2 * n + d] = dot(prod[1], dm3.astype(BF16), 0, 0).astype(BF16)
     else:
         for i in range(hops):
             dm_refs[0][i] = grads[i]
@@ -182,15 +186,13 @@
 
 
 def finish(own_ref, *refs, n):
-    back = (refs[0:3], refs[3:6])
-    outs = refs[6:8]
-    wide = refs[8]
+    back, outs, wide = (refs[0:3], refs[3:6]), refs[6:8], refs[8]
     for part in range(2):
-        lo, hi = part * n, (part + 1) * n
+        rows = slice(part * n, (part + 1) * n)
         for g in range(2):
-            total = own_ref[g, lo:hi]
-            for b in back[g]:
-                total = total + b[lo:hi].astype(F32)
+            total = own_ref[g, rows]
+            for ref in back[g]:
+                total = total + ref[rows].astype(F32)
             wide[pl.ds(g, n, stride=2)] = total
         outs[part][...] = wide[...].astype(BF16)
 
@@ -218,7 +220,7 @@
     buf_a, buf_b, own = pl.pallas_call(
         functools.partial(prepare, n=n),
         out_shape=[
-            jax.ShapeDtypeStruct((2 * n + 2 * d, d), BF16),
+            jax.ShapeDtypeStruct((2 * n + d, d), BF16),
             jax.ShapeDtypeStruct((2 * n, d), BF16),
             jax.ShapeDtypeStruct((kv, 2 * n, d), BF16),
         ],
@@ -226,10 +228,9 @@
         name="prepare",
     )(key_heads.reshape(2 * n, d), value_heads.reshape(2 * n, d), transforms[0])
 
-    arr_a = []
+    arr_a, arr_b = [], []
     for h in range(1, HOPS + 1):
         arr_a.append(shift(buf_a, h))
-
     rows_blk = pl.BlockSpec((n, None, group, d), lambda g: (0, g, 0, 0))
     own_blk = pl.BlockSpec((None, 2 * n, d), lambda g: (g, 0, 0))
     stat_blk = pl.BlockSpec((None, 8, R), lambda g: (g, 0, 0))
@@ -243,20 +244,19 @@
         name="near_stats",
     )(q4, do4, own)
 
-    buf_b, *arr_a = lax.optimization_barrier((buf_b, *arr_a))
-    arr_b = []
+    buf_b, stats0 = lax.optimization_barrier((buf_b, stats0))
     for h in range(1, HOPS + 1):
         arr_b.append(shift(buf_b, h))
 
     def call(head, arrived, extra):
-        blk = pl.BlockSpec((n, None, group, d), lambda c, *s: (0, head, 0, 0))
         st = pl.BlockSpec((None, 8, R), lambda c, *s: (head, 0, 0))
-        turn_spec = pl.BlockSpec((2 * d, d), lambda c, *s: (n // d, 0))
+        turn_spec = pl.BlockSpec((d, d), lambda c, *s: (2 * n // d, 0))
         row_spec = pl.BlockSpec((2 * n, d), lambda c, *s: (0, 0))
-        in_specs = [blk, blk] + [row_spec] * HOPS + [turn_spec] * HOPS + [st]
+        raw = pl.BlockSpec(memory_space=pl.ANY)
+        in_specs = [raw, raw] + [row_spec] * HOPS + [turn_spec] * HOPS + [st]
         args = [q4, do4, *arrived, *arr_a, stats0]
         alias = {}
-        dms = [jax.ShapeDtypeStruct((d, d), BF16)] * HOPS
+        dms = []
         if head:
             prev_dq, prev_st, prev_dm = extra
             in_specs += [whole(prev_dm.shape)] + [pl.BlockSpec(memory_space=pl.ANY)] * 2
@@ -264,7 +264,7 @@
             alias = {len(args): 0, len(args) + 1: 1}
         else:
             dms = [jax.ShapeDtypeStruct((HOPS, d, d), F32)]
-        yshape = jax.ShapeDtypeStruct((2 * n, d), BF16)
+        yshape = jax.ShapeDtypeStruct((2 * n + head * d, d), BF16)
         return pl.pallas_call(
             functools.partial(
                 far,
@@ -275,10 +275,10 @@
                 grid=(1,),
                 in_specs=in_specs,
                 out_specs=[pl.BlockSpec((None, d, R), lambda c, *s: (head, 0, 0)), st]
-                + [whole((2 * n, d))] * HOPS
+                + [whole(yshape.shape)] * HOPS
                 + [whole(x.shape) for x in dms],
                 scratch_shapes=[
-                    pltpu.VMEM((HOPS, d, d), F32),
+                    pltpu.VMEM((HOPS, d, d), BF16),
                     pltpu.VMEM((HOPS, n, d), BF16),
                     pltpu.VMEM((HOPS, n, d), BF16),
                     pltpu.VMEM((HOPS, d, n), BF16),
@@ -287,6 +287,9 @@
                     pltpu.VMEM((HOPS, n, R), F32),
                     pltpu.VMEM((HOPS, n, R), F32),
                     pltpu.VMEM((HOPS, 1, R), F32),
+                    pltpu.VMEM((n, group, d), BF16),
+                    pltpu.VMEM((n, group, d), BF16),
+                    pltpu.SemaphoreType.DMA((2,)),
                 ],
             ),
             out_shape=[
@@ -295,7 +298,7 @@
                 yshape, yshape, yshape, *dms,
             ],
             input_output_aliases=alias,
-            compiler_params=pltpu.CompilerParams(vmem_limit_bytes=56 << 20),
+            compiler_params=pltpu.CompilerParams(vmem_limit_bytes=48 << 20),
             cost_estimate=cost(9_000_000_000, 6_000_000),
         )(window, first_block, *args)
 
@@ -303,11 +306,9 @@
     back_a = []
     for h in range(HOPS):
         back_a.append(shift(ys_a[h], -h - 1))
-    dq, st, y1, y2, y3, *dms = call(1, arr_b, (dq, st, dm_a))
-    dt, back_b = [], []
-    for h in range(HOPS):
-        dt.append(shift(dms[h], -h - 1))
-    for h, y in enumerate((y1, y2, y3)):
+    dq, st, *ys_b = call(1, arr_b, (dq, st, dm_a))
+    back_b = []
+    for h, y in enumerate(ys_b):
         back_b.append(shift(y, -h - 1))
 
     dq_out, own_grad = pl.pallas_call(
@@ -323,7 +324,8 @@
         name="near",
     )(q4, do4, own, st, dq)
 
-    turn = dt[0].astype(F32) + dt[1].astype(F32) + dt[2].astype(F32)
+    dt = [b[2 * n :].astype(F32) for b in back_b]
+    turn = lax.optimization_barrier(sum(dt[1:], dt[0]))
     peers = lax.axis_size("kv")
     half = turn.astype(BF16)
     total = turn
@@ -335,6 +337,7 @@
         functools.partial(finish, n=n),
         out_shape=[jax.ShapeDtypeStruct((2 * n, d), BF16)] * 2,
         scratch_shapes=[pltpu.VMEM((2 * n, d), F32)],
+        cost_estimate=cost(1_000_000, 3_000_000),
         name="finish",
     )(own_grad, *back_a, *back_b)
     return (

time: 120 us -> 96.6 us (0.80)
  the two profiles are of different devices: /device:TPU:14 before, /device:TPU:31 now
where the time goes in v1:
time: 96.6 us; the launch traced here: 96.3 us
  starting transfers between devices  36.8 us (38%)
  Pallas kernels  34.6 us (36%)
  waiting for transfers between devices  21.1 us (22%)
  local copies, waits for them, and re-layouts  1.72 us (2%)
  between operations  1.45 us (2%)
    ppermute x3, starting transfers between devices, shards(): lax.ppermute(half, 'kv', [(i, (i + k) % peers) for i in range(peers)])  21.9 us
    ppermute x12, waiting for transfers between devices, shift(): return lax.ppermute(x, 'ctx', [(i, (i + by) % n) for i in range(n)])  21.1 us
    pallas_call x2, Pallas kernels, call(): pl.pallas_call(functools.partial(far, head=head, n=n, d=d, hops=HOPS, c2=...  18.1 us
    ppermute x12, starting transfers between devices, shift(): return lax.ppermute(x, 'ctx', [(i, (i + by) % n) for i in range(n)])  14.9 us
    pallas_call x1, Pallas kernels, shards(): pl.pallas_call(functools.partial(near, n=n, d=d, cut=cut, c2=c2, factor=f...  7.38 us
    pallas_call x1, Pallas kernels, shards(): pl.pallas_call(functools.partial(near_stats, n=n, d=d, cut=cut, c2=c2), g...  4.57 us
    pallas_call x1, Pallas kernels, shards(): pl.pallas_call(functools.partial(finish, n=n), out_shape=[jax.ShapeDtypeS...  2.51 us
    pallas_call x1, Pallas kernels, shards(): pl.pallas_call(functools.partial(prepare, n=n), out_shape=[jax.ShapeDtype...  2.02 us
  transfers between devices with their start and end apart: 15, of which 4 were waited for; matrix products, arithmetic and copies ran while one was open for 0% of the time, Pallas kernels for 26%

profile of v1, /device:TPU:31, one launch (start us, length us, event | category | flops | bytes accessed | tf_op | source)
XLA Modules:
  0.0 96.3 jit_solution(17486282286712603497)
XLA Ops:
  0.6 2.0 %prepare.1 = (bf16[896,128]{1,0:T(8,128)(2,1)}, bf16[768,128]{1,0:T(8,128)(2,1)}, bf16[2,768,128]{2,1,0:T(8,128)(2,1)}) custom-call(bf16[768,128]{1,0:T(8,128)(2,1)} %bitcast.18, bf16[768,128]{1,0:T(8,128)(2,1)} %bitcast.19, f32[128,128]{1,0:T(8,128)} %bitcast.20), custom_call_target="tpu_custom_call" | custom-call | tf_op jit(solution)/shard_map/prepare/pallas_call | solution.py:220
  2.7 3.7 %collective-permute-start.5 = (bf16[896,128]{1,0:T(8,128)(2,1)}, bf16[896,128]{1,0:T(8,128)(2,1)S(1)}, u32[]{:S(2)}, u32[]{:S(2)}) collective-permute-start(bf16[896,128]{1,0:T(8,128)(2,1)} %get-tuple-element.27), channel_id=1, source_target_pairs={{0,12},{4,16},{8,20},{12,24},{16,28},{20,32},{24,36},{28,40},{32,4... | collective-permute-start | bytes 688136 | tf_op jit(solution)/shard_map/ppermute | solution.py:33
  6.3 1.6 %collective-permute-start.4 = (bf16[896,128]{1,0:T(8,128)(2,1)}, bf16[896,128]{1,0:T(8,128)(2,1)}, u32[]{:S(2)}, u32[]{:S(2)}) collective-permute-start(bf16[896,128]{1,0:T(8,128)(2,1)} %get-tuple-element.27), channel_id=1, source_target_pairs={{0,8},{4,12},{8,16},{12,20},{16,24},{20,28},{24,32},{28,36},{32,40... | collective-permute-start | bytes 688136 | tf_op jit(solution)/shard_map/ppermute | solution.py:33
  7.9 1.9 %collective-permute-start.3 = (bf16[896,128]{1,0:T(8,128)(2,1)}, bf16[896,128]{1,0:T(8,128)(2,1)}, u32[]{:S(2)}, u32[]{:S(2)}) collective-permute-start(bf16[896,128]{1,0:T(8,128)(2,1)} %get-tuple-element.27), channel_id=1, source_target_pairs={{0,4},{4,8},{8,12},{12,16},{16,20},{20,24},{24,28},{28,32},{32,36}... | collective-permute-start | bytes 688136 | tf_op jit(solution)/shard_map/ppermute | solution.py:33
  9.8 4.6 %near_stats.1.near_ref = f32[2,8,3072]{2,1,0:T(8,128)} custom-call(bf16[384,2,8,128]{3,2,1,0:T(8,128)(2,1)} %bitcast.10, bf16[384,2,8,128]{3,2,1,0:T(8,128)(2,1)} %bitcast.14, bf16[2,768,128]{2,1,0:T(8,128)(2,1)} %get-tuple-element.24.own_ref), custom_call_target="tpu_custom_call" | custom-call | flops 2500000000 | bytes 6000000 | tf_op jit(solution)/shard_map/near_stats/pallas_call | solution.py:237
  14.4 0.5 collective-permute-start.2
  14.9 2.3 %collective-permute-start.1 = (bf16[768,128]{1,0:T(8,128)(2,1)}, bf16[768,128]{1,0:T(8,128)(2,1)S(1)}, u32[]{:S(2)}, u32[]{:S(2)}) collective-permute-start(bf16[768,128]{1,0:T(8,128)(2,1)} %get-tuple-element.26), channel_id=1, source_target_pairs={{0,8},{4,12},{8,16},{12,20},{16,24},{20,28},{24,32},{28,36},{32,40... | collective-permute-start | bytes 589832 | tf_op jit(solution)/shard_map/ppermute | solution.py:33
  17.9 2.3 %collective-permute-start = (bf16[768,128]{1,0:T(8,128)(2,1)}, bf16[768,128]{1,0:T(8,128)(2,1)S(1)}, u32[]{:S(2)}, u32[]{:S(2)}) collective-permute-start(bf16[768,128]{1,0:T(8,128)(2,1)} %get-tuple-element.26), channel_id=1, source_target_pairs={{0,4},{4,8},{8,12},{12,16},{16,20},{20,24},{24,28},{28,32},{32,36}... | collective-permute-start | bytes 589832 | tf_op jit(solution)/shard_map/ppermute | solution.py:33
  20.2 1.7 %collective-permute-done.3.r1_ref.t1_ref = bf16[896,128]{1,0:T(8,128)(2,1)} collective-permute-done((bf16[896,128]{1,0:T(8,128)(2,1)}, bf16[896,128]{1,0:T(8,128)(2,1)}, u32[]{:S(2)}, u32[]{:S(2)}) %collective-permute-start.3) | collective-permute-done | bytes 229408 | tf_op jit(solution)/shard_map/ppermute | solution.py:33
  21.9 0.9 copy-done.3
  22.9 10.8 %shard_map.102 = (f32[2,128,3072]{2,1,0:T(8,128)}, f32[2,8,3072]{2,1,0:T(8,128)S(1)}, bf16[768,128]{1,0:T(8,128)(2,1)S(1)}, bf16[768,128]{1,0:T(8,128)(2,1)}, bf...) custom-call(s32[2]{0:T(128)S(1)} %copy-done.2, s32[1]{0:T(128)S(6)} %copy.15.fst, ...), custom_call_target="tpu_custom_call" | custom-call | flops 8999999488 | bytes 6000000 | tf_op jit(solution)/shard_map/pallas_call | solution.py:268
  33.7 1.1 %collective-permute-done.r1_ref = bf16[768,128]{1,0:T(8,128)(2,1)S(1)} collective-permute-done((bf16[768,128]{1,0:T(8,128)(2,1)}, bf16[768,128]{1,0:T(8,128)(2,1)S(1)}, u32[]{:S(2)}, u32[]{:S(2)}) %collective-permute-start) | collective-permute-done | bytes 196640 | tf_op jit(solution)/shard_map/ppermute | solution.py:33
  34.8 7.3 %shard_map.103 = (f32[2,128,3072]{2,1,0:T(8,128)}, f32[2,8,3072]{2,1,0:T(8,128)S(1)}, bf16[896,128]{1,0:T(8,128)(2,1)S(1)}, bf16[896,128]{1,0:T(8,128)(2,1)S(1)}, bf16[896,128]{1,0:T(8,128)(2,1)S(1)}) custom-call(s32[2]{0:T(128)S(1)} %copy-done.2, s32[1]{0:T(128)S(6)} %copy.15.fst, ...), custom_call_target="tpu_custom_call", output_to_operand_aliasing={{0}: (12, {}), {1}: (13, {})} | custom-call | flops 8999999488 | bytes 6000000 | tf_op jit(solution)/shard_map/pallas_call | solution.py:268
  42.2 0.9 collective-permute-start.10
  43.1 1.6 %collective-permute-start.6 = (bf16[768,128]{1,0:T(8,128)(2,1)S(1)}, bf16[768,128]{1,0:T(8,128)(2,1)S(1)}, u32[]{:S(2)}, u32[]{:S(2)}) collective-permute-start(bf16[768,128]{1,0:T(8,128)(2,1)S(1)} %get-tuple-element.36), channel_id=1, source_target_pairs={{0,124},{4,0},{8,4},{12,8},{16,12},{20,16},{24,20},{28,24},{32,28}... | collective-permute-start | bytes 589832 | tf_op jit(solution)/shard_map/ppermute | solution.py:33
  44.7 14.6 %collective-permute-done.9.refs_3_ = bf16[896,128]{1,0:T(8,128)(2,1)S(1)} collective-permute-done((bf16[896,128]{1,0:T(8,128)(2,1)S(1)}, bf16[896,128]{1,0:T(8,128)(2,1)S(1)}, u32[]{:S(2)}, u32[]{:S(2)}) %collective-permute-start.9) | collective-permute-done | bytes 229408 | tf_op jit(solution)/shard_map/ppermute | solution.py:33
  59.4 3.6 %collective-permute-done.10.refs_4_ = bf16[896,128]{1,0:T(8,128)(2,1)S(1)} collective-permute-done((bf16[896,128]{1,0:T(8,128)(2,1)S(1)}, bf16[896,128]{1,0:T(8,128)(2,1)S(1)}, u32[]{:S(2)}, u32[]{:S(2)}) %collective-permute-start.10) | collective-permute-done | bytes 229408 | tf_op jit(solution)/shard_map/ppermute | solution.py:33
  63.0 8.3 %collective-permute-start.14 = (bf16[128,128]{1,0:T(8,128)(2,1)S(1)}, bf16[128,128]{1,0:T(8,128)(2,1)S(1)}, u32[]{:S(2)}, u32[]{:S(2)}) collective-permute-start(bf16[128,128]{1,0:T(8,128)(2,1)S(1)} %convert_element_type.24), channel_id=1, source_target_pairs={{0,3},{1,0},{2,1},{3,2},{4,7},{5,4},{6,5},{7,6},{8,11},{9,8},{10,9... | collective-permute-start | bytes 98312 | tf_op jit(solution)/shard_map/ppermute | solution.py:333
  71.3 8.5 %collective-permute-start.13 = (bf16[128,128]{1,0:T(8,128)(2,1)S(1)}, bf16[128,128]{1,0:T(8,128)(2,1)S(1)}, u32[]{:S(2)}, u32[]{:S(2)}) collective-permute-start(bf16[128,128]{1,0:T(8,128)(2,1)S(1)} %convert_element_type.24), channel_id=1, source_target_pairs={{0,2},{1,3},{2,0},{3,1},{4,6},{5,7},{6,4},{7,5},{8,10},{9,11},{10,... | collective-permute-start | bytes 98312 | tf_op jit(solution)/shard_map/ppermute | solution.py:333
  79.8 5.1 %collective-permute-start.12 = (bf16[128,128]{1,0:T(8,128)(2,1)S(1)}, bf16[128,128]{1,0:T(8,128)(2,1)S(1)}, u32[]{:S(2)}, u32[]{:S(2)}) collective-permute-start(bf16[128,128]{1,0:T(8,128)(2,1)S(1)} %convert_element_type.24), channel_id=1, source_target_pairs={{0,1},{1,2},{2,3},{3,0},{4,5},{5,6},{6,7},{7,4},{8,9},{9,10},{10,1... | collective-permute-start | bytes 98312 | tf_op jit(solution)/shard_map/ppermute | solution.py:333
  84.9 7.4 %near.1 = (bf16[384,2,8,128]{3,2,1,0:T(8,128)(2,1)}, f32[2,768,128]{2,1,0:T(8,128)}) custom-call(bf16[384,2,8,128]{3,2,1,0:T(8,128)(2,1)} %bitcast.11, bf16[384,2,8,128]{3,2,1,0:T(8,128)(2,1)} %bitcast.15, bf16[2,768,128]{2,1,0:T(8,128)(2,1)} %get-tuple-element.24.own_ref, f32[2,8,3072]{2,1,0:T(8,128)} %copy-done.5, f32[2,128,3072]{2,1,0:T(8,128)} %get-tuple-element.33.far_ref), custom_call_target="tpu_custom_call" | custom-call | flops 5000000000 | bytes 9000000 | tf_op jit(solution)/shard_map/near/pallas_call | solution.py:314
  92.4 0.6 copy-done.10
  93.1 2.5 %finish.1 = (bf16[768,128]{1,0:T(8,128)(2,1)}, bf16[768,128]{1,0:T(8,128)(2,1)}) custom-call(f32[2,768,128]{2,1,0:T(8,128)} %get-tuple-element.35.own_ref, bf16[768,128]{1,0:T(8,128)(2,1)} %copy-done.9, bf16[768,128]{1,0:T(8,128)(2,1)} %copy-done.10, bf16[768,128]{1,0:T(8,128)(2,1)} %copy-done.11, bf16[896,128]{1,0:T(8,128)(2,1)} %copy-done.6, ...), custom_call_target="tpu_custom_call" | custom-call | flops 1000000 | bytes 3000000 | tf_op jit(solution)/shard_map/finish/pallas_call | solution.py:336
  95.7 0.6 add_bitcast_fusion
  (39 shorter events, 0.3 us)
Async XLA Ops:
  2.7 15.2 %collective-permute-start.5 = (bf16[896,128]{1,0:T(8,128)(2,1)}, bf16[896,128]{1,0:T(8,128)(2,1)S(1)}, u32[]{:S(2)}, u32[]{:S(2)}) collective-permute-start(bf16[896,128]{1,0:T(8,128)(2,1)} %get-tuple-element.27), channel_id=1, source_target_pairs={{0,12},{4,16},{8,20},{12,24},{16,28},{20,32},{24,36},{28,40},{32,4... | collective-permute-start | bytes 688136 | tf_op jit(solution)/shard_map/ppermute | solution.py:33
  6.3 13.8 %collective-permute-start.4 = (bf16[896,128]{1,0:T(8,128)(2,1)}, bf16[896,128]{1,0:T(8,128)(2,1)}, u32[]{:S(2)}, u32[]{:S(2)}) collective-permute-start(bf16[896,128]{1,0:T(8,128)(2,1)} %get-tuple-element.27), channel_id=1, source_target_pairs={{0,8},{4,12},{8,16},{12,20},{16,24},{20,28},{24,32},{28,36},{32,40... | collective-permute-start | bytes 688136 | tf_op jit(solution)/shard_map/ppermute | solution.py:33
  7.9 14.0 %collective-permute-start.3 = (bf16[896,128]{1,0:T(8,128)(2,1)}, bf16[896,128]{1,0:T(8,128)(2,1)}, u32[]{:S(2)}, u32[]{:S(2)}) collective-permute-start(bf16[896,128]{1,0:T(8,128)(2,1)} %get-tuple-element.27), channel_id=1, source_target_pairs={{0,4},{4,8},{8,12},{12,16},{16,20},{20,24},{24,28},{28,32},{32,36}... | collective-permute-start | bytes 688136 | tf_op jit(solution)/shard_map/ppermute | solution.py:33
  9.8 12.1 %copy-start = (bf16[384,16,128]{2,1,0:T(8,128)(2,1)S(1)}, bf16[384,16,128]{2,1,0:T(8,128)(2,1)}, u32[]{:S(2)}) copy-start(bf16[384,16,128]{2,1,0:T(8,128)(2,1)} %param.7) | copy-start | bytes 4718596
  9.8 12.1 %copy-start.1 = (bf16[384,16,128]{2,1,0:T(8,128)(2,1)S(1)}, bf16[384,16,128]{2,1,0:T(8,128)(2,1)}, u32[]{:S(2)}) copy-start(bf16[384,16,128]{2,1,0:T(8,128)(2,1)} %param.10) | copy-start | bytes 4718596
  9.8 12.1 %copy-start.2 = (s32[2]{0:T(128)S(1)}, s32[2]{0:T(128)}, u32[]{:S(2)}) copy-start(s32[2]{0:T(128)} %win.3) | copy-start | bytes 28
  14.4 19.3 %collective-permute-start.2 = (bf16[768,128]{1,0:T(8,128)(2,1)}, bf16[768,128]{1,0:T(8,128)(2,1)S(1)}, u32[]{:S(2)}, u32[]{:S(2)}) collective-permute-start(bf16[768,128]{1,0:T(8,128)(2,1)} %get-tuple-element.26), channel_id=1, source_target_pairs={{0,12},{4,16},{8,20},{12,24},{16,28},{20,32},{24,36},{28,40},{32,4... | collective-permute-start | bytes 589832 | tf_op jit(solution)/shard_map/ppermute | solution.py:33
  14.9 18.8 %collective-permute-start.1 = (bf16[768,128]{1,0:T(8,128)(2,1)}, bf16[768,128]{1,0:T(8,128)(2,1)S(1)}, u32[]{:S(2)}, u32[]{:S(2)}) collective-permute-start(bf16[768,128]{1,0:T(8,128)(2,1)} %get-tuple-element.26), channel_id=1, source_target_pairs={{0,8},{4,12},{8,16},{12,20},{16,24},{20,28},{24,32},{28,36},{32,40... | collective-permute-start | bytes 589832 | tf_op jit(solution)/shard_map/ppermute | solution.py:33
  17.9 16.9 %collective-permute-start = (bf16[768,128]{1,0:T(8,128)(2,1)}, bf16[768,128]{1,0:T(8,128)(2,1)S(1)}, u32[]{:S(2)}, u32[]{:S(2)}) collective-permute-start(bf16[768,128]{1,0:T(8,128)(2,1)} %get-tuple-element.26), channel_id=1, source_target_pairs={{0,4},{4,8},{8,12},{12,16},{16,20},{20,24},{24,28},{28,32},{32,36}... | collective-permute-start | bytes 589832 | tf_op jit(solution)/shard_map/ppermute | solution.py:33
  22.9 11.9 %copy-start.4 = (f32[2,8,3072]{2,1,0:T(8,128)S(1)}, f32[2,8,3072]{2,1,0:T(8,128)}, u32[]{:S(2)}) copy-start(f32[2,8,3072]{2,1,0:T(8,128)} %near_stats.1.near_ref) | copy-start | bytes 589828
  42.1 37.7 %copy-start.5 = (f32[2,8,3072]{2,1,0:T(8,128)}, f32[2,8,3072]{2,1,0:T(8,128)S(1)}, u32[]{:S(2)}) copy-start(f32[2,8,3072]{2,1,0:T(8,128)S(1)} %get-tuple-element.32.stat_ref) | copy-start | bytes 589828
  42.1 17.3 %collective-permute-start.9 = (bf16[896,128]{1,0:T(8,128)(2,1)S(1)}, bf16[896,128]{1,0:T(8,128)(2,1)S(1)}, u32[]{:S(2)}, u32[]{:S(2)}) collective-permute-start(bf16[896,128]{1,0:T(8,128)(2,1)S(1)} %get-tuple-element.39), channel_id=1, source_target_pairs={{0,124},{4,0},{8,4},{12,8},{16,12},{20,16},{24,20},{28,24},{32,28}... | collective-permute-start | bytes 688136 | tf_op jit(solution)/shard_map/ppermute | solution.py:33
  42.2 20.8 %collective-permute-start.10 = (bf16[896,128]{1,0:T(8,128)(2,1)S(1)}, bf16[896,128]{1,0:T(8,128)(2,1)S(1)}, u32[]{:S(2)}, u32[]{:S(2)}) collective-permute-start(bf16[896,128]{1,0:T(8,128)(2,1)S(1)} %get-tuple-element.40), channel_id=1, source_target_pairs={{0,120},{4,124},{8,0},{12,4},{16,8},{20,12},{24,16},{28,20},{32,24... | collective-permute-start | bytes 688136 | tf_op jit(solution)/shard_map/ppermute | solution.py:33
  43.1 19.9 %collective-permute-start.11 = (bf16[896,128]{1,0:T(8,128)(2,1)S(1)}, bf16[896,128]{1,0:T(8,128)(2,1)S(1)}, u32[]{:S(2)}, u32[]{:S(2)}) collective-permute-start(bf16[896,128]{1,0:T(8,128)(2,1)S(1)} %get-tuple-element.41), channel_id=1, source_target_pairs={{0,116},{4,120},{8,124},{12,0},{16,4},{20,8},{24,12},{28,16},{32,2... | collective-permute-start | bytes 688136 | tf_op jit(solution)/shard_map/ppermute | solution.py:33
  43.1 36.7 %collective-permute-start.6 = (bf16[768,128]{1,0:T(8,128)(2,1)S(1)}, bf16[768,128]{1,0:T(8,128)(2,1)S(1)}, u32[]{:S(2)}, u32[]{:S(2)}) collective-permute-start(bf16[768,128]{1,0:T(8,128)(2,1)S(1)} %get-tuple-element.36), channel_id=1, source_target_pairs={{0,124},{4,0},{8,4},{12,8},{16,12},{20,16},{24,20},{28,24},{32,28}... | collective-permute-start | bytes 589832 | tf_op jit(solution)/shard_map/ppermute | solution.py:33
  44.7 47.6 %collective-permute-start.7 = (bf16[768,128]{1,0:T(8,128)(2,1)}, bf16[768,128]{1,0:T(8,128)(2,1)S(1)}, u32[]{:S(2)}, u32[]{:S(2)}) collective-permute-start(bf16[768,128]{1,0:T(8,128)(2,1)} %get-tuple-element.37), channel_id=1, source_target_pairs={{0,120},{4,124},{8,0},{12,4},{16,8},{20,12},{24,16},{28,20},{32,24... | collective-permute-start | bytes 589832 | tf_op jit(solution)/shard_map/ppermute | solution.py:33
  59.4 32.9 %copy-start.6 = (bf16[896,128]{1,0:T(8,128)(2,1)}, bf16[896,128]{1,0:T(8,128)(2,1)S(1)}, u32[]{:S(2)}) copy-start(bf16[896,128]{1,0:T(8,128)(2,1)S(1)} %collective-permute-done.9.refs_3_) | copy-start | bytes 688132
  59.4 33.0 %collective-permute-start.8 = (bf16[768,128]{1,0:T(8,128)(2,1)}, bf16[768,128]{1,0:T(8,128)(2,1)S(1)}, u32[]{:S(2)}, u32[]{:S(2)}) collective-permute-start(bf16[768,128]{1,0:T(8,128)(2,1)} %get-tuple-element.38), channel_id=1, source_target_pairs={{0,116},{4,120},{8,124},{12,0},{16,4},{20,8},{24,12},{28,16},{32,2... | collective-permute-start | bytes 589832 | tf_op jit(solution)/shard_map/ppermute | solution.py:33
  63.0 29.3 %copy-start.7 = (bf16[896,128]{1,0:T(8,128)(2,1)}, bf16[896,128]{1,0:T(8,128)(2,1)S(1)}, u32[]{:S(2)}) copy-start(bf16[896,128]{1,0:T(8,128)(2,1)S(1)} %collective-permute-done.10.refs_4_) | copy-start | bytes 688132
  63.0 29.4 %copy-start.8 = (bf16[896,128]{1,0:T(8,128)(2,1)}, bf16[896,128]{1,0:T(8,128)(2,1)S(1)}, u32[]{:S(2)}) copy-start(bf16[896,128]{1,0:T(8,128)(2,1)S(1)} %collective-permute-done.11.refs_5_) | copy-start | bytes 688132
  63.0 32.6 %collective-permute-start.14 = (bf16[128,128]{1,0:T(8,128)(2,1)S(1)}, bf16[128,128]{1,0:T(8,128)(2,1)S(1)}, u32[]{:S(2)}, u32[]{:S(2)}) collective-permute-start(bf16[128,128]{1,0:T(8,128)(2,1)S(1)} %convert_element_type.24), channel_id=1, source_target_pairs={{0,3},{1,0},{2,1},{3,2},{4,7},{5,4},{6,5},{7,6},{8,11},{9,8},{10,9... | collective-permute-start | bytes 98312 | tf_op jit(solution)/shard_map/ppermute | solution.py:333
  71.3 24.4 %collective-permute-start.13 = (bf16[128,128]{1,0:T(8,128)(2,1)S(1)}, bf16[128,128]{1,0:T(8,128)(2,1)S(1)}, u32[]{:S(2)}, u32[]{:S(2)}) collective-permute-start(bf16[128,128]{1,0:T(8,128)(2,1)S(1)} %convert_element_type.24), channel_id=1, source_target_pairs={{0,2},{1,3},{2,0},{3,1},{4,6},{5,7},{6,4},{7,5},{8,10},{9,11},{10,... | collective-permute-start | bytes 98312 | tf_op jit(solution)/shard_map/ppermute | solution.py:333
  79.8 12.5 %copy-start.9 = (bf16[768,128]{1,0:T(8,128)(2,1)}, bf16[768,128]{1,0:T(8,128)(2,1)S(1)}, u32[]{:S(2)}) copy-start(bf16[768,128]{1,0:T(8,128)(2,1)S(1)} %collective-permute-done.6.refs_0_) | copy-start | bytes 589828
  79.8 15.8 %collective-permute-start.12 = (bf16[128,128]{1,0:T(8,128)(2,1)S(1)}, bf16[128,128]{1,0:T(8,128)(2,1)S(1)}, u32[]{:S(2)}, u32[]{:S(2)}) collective-permute-start(bf16[128,128]{1,0:T(8,128)(2,1)S(1)} %convert_element_type.24), channel_id=1, source_target_pairs={{0,1},{1,2},{2,3},{3,0},{4,5},{5,6},{6,7},{7,4},{8,9},{9,10},{10,1... | collective-permute-start | bytes 98312 | tf_op jit(solution)/shard_map/ppermute | solution.py:333
  (3 other events, 2.4 us)
